TPU v7x, 32 devices: a whole 2x2x4 slice. The times are simulated.
32 devices in a mesh: ctx: 8 (over z, y), head: 4 (over x, core).
Axes of the slice: x: 2, y: 2, z: 4, core: 2. Of those that a mesh axis runs over, the one named last changes fastest.
Arguments:
- query_all: bfloat16 [1024, 1024], P('ctx', 'head'), may hold values from -6 to 6
- key_all: bfloat16 [1024, 1024], P('ctx', 'head'), may hold values from -6 to 6
- value_all: bfloat16 [1024, 1024], P('ctx', 'head'), may hold values from -6 to 6
- cotangent: bfloat16 [1024, 1024], P('ctx', 'head'), may hold values from -6 to 6
- conv_input: bfloat16 [1024, 1024], P('ctx', 'head'), may hold values from -6 to 6
- rec_lengths: int32 [3], replicated, may hold values from 170 to 341
- out_proj: bfloat16 [1024, 1024], P(None, 'head'), may hold values from -0.1875 to 0.1875
- conv_weight: bfloat16 [31, 1024], P(None, 'head'), may hold values from -1 to 1
Outputs:
- q_grad: bfloat16 [1024, 1024], P('ctx', 'head')
- k_grad: bfloat16 [1024, 1024], P('ctx', 'head')
- v_grad: bfloat16 [1024, 1024], P('ctx', 'head')
- x_grad: bfloat16 [1024, 1024], P('ctx', 'head')
- out_proj_grad: float32 [1024, 1024], P('ctx', 'head')
- conv_weight_grad: float32 [31, 1024], P(None, 'head')
Inputs may be any that keep to these rules, and one draw needn't show every extreme that they name: `rec_lengths`: the recordings lie end to end from frame 0; frames from their total on are padding.
All inputs are finite; a program needn't handle non-finite values.
Results may differ from a plain program's by a relative error of at most 0.03.
Values may be sent and summed in bfloat16 or wider, within the bound.
No kernel may reach another device: no remote copies, remote signals or barrier semaphores. Data moves between devices by JAX's collectives and lax.ppermute only.
A program may use at most 64 MiB of HBM per device.

v0:
```python
import jax
import jax.numpy as jnp
from jax import lax
from jax.sharding import PartitionSpec as P

HEAD_DIM = 64


def extended_2(block, sides, width):
    for axis, dim in sides:
        count = lax.axis_size(axis)
        forward = [(i, i + 1) for i in range(count - 1)]
        backward = [(target, source) for source, target in forward]
        low = lax.ppermute(
            lax.slice_in_dim(block, block.shape[dim] - width, None, axis=dim), axis, forward
        )
        high = lax.ppermute(lax.slice_in_dim(block, 0, width, axis=dim), axis, backward)
        block = jnp.concatenate([low, block, high], axis=dim)
    return block


def split_heads(matrix):
    return matrix.reshape(matrix.shape[0], -1, HEAD_DIM)


def join_heads(tensor):
    return jnp.transpose(tensor, (1, 0, 2)).reshape(tensor.shape[1], -1)


def over_blocks(step_fn, running, members):
    row_count = members[0].shape[0]
    blocks = row_count // 512
    stacked = tuple((member.reshape((blocks, 512) + member.shape[1:]) for member in members))

    def inner_step(state, inputs):
        block_members, block_index = inputs
        return (step_fn(state, block_members, block_index * 512), None)

    running, unused = lax.scan(inner_step, running, (stacked, jnp.arange(blocks, dtype=jnp.int32)))
    return running


def conv_forward(extended, taps, frames):
    wide = extended.astype(jnp.float32)
    weights = taps.astype(jnp.float32)
    result = jnp.zeros((frames, extended.shape[1]), jnp.float32)
    for offset in range(taps.shape[0]):
        result = result + weights[offset] * wide[offset : offset + frames]
    return result


def conv_backward(grad_ext, taps, frames):
    wide = grad_ext.astype(jnp.float32)
    weights = taps.astype(jnp.float32)
    reach = taps.shape[0] - 1
    result = jnp.zeros((frames, grad_ext.shape[1]), jnp.float32)
    for offset in range(taps.shape[0]):
        result = result + weights[offset] * wide[reach - offset : reach - offset + frames]
    return result


def tap_products(grad_conv, extended):
    frames = grad_conv.shape[0]
    wide = extended.astype(jnp.float32)
    grad_wide = grad_conv.astype(jnp.float32)
    rows_out = [
        jnp.sum(grad_wide * wide[offset : offset + frames], axis=0)
        for offset in range(extended.shape[0] - frames + 1)
    ]
    return jnp.stack(rows_out)


def gate_slope(conv_out, upstream):
    sigmoid_value = jax.nn.sigmoid(conv_out)
    return (
        upstream.astype(jnp.float32) * sigmoid_value * (1.0 + conv_out * (1.0 - sigmoid_value))
    ).astype(jnp.bfloat16)


def on_device(
    query_all, key_all, value_all, cotangent, conv_input, rec_lengths, out_proj, conv_weight
):
    frames, local_width = query_all.shape
    half_taps = conv_weight.shape[0] // 2
    score_scale = HEAD_DIM ** (-0.5)
    valid_total = jnp.sum(rec_lengths)
    positions = lax.axis_index("ctx") * frames + jnp.arange(frames, dtype=jnp.int32)
    frame_ok = positions < valid_total
    masked = jnp.where(frame_ok[:, None], conv_input, jnp.zeros_like(conv_input))
    input_ext = extended_2(masked, (("ctx", 0),), half_taps)
    conv_out = conv_forward(input_ext, conv_weight, frames)
    grad_conv = gate_slope(conv_out, cotangent)
    grad_ext = extended_2(grad_conv, (("ctx", 0),), half_taps)
    conv_weight_grad = lax.psum(tap_products(grad_conv, input_ext), "ctx")
    grad_input = conv_backward(grad_ext, conv_weight, frames)
    x_grad = (cotangent.astype(jnp.float32) + jnp.where(frame_ok[:, None], grad_input, 0.0)).astype(
        jnp.bfloat16
    )
    full_grad = lax.all_gather(x_grad, "head", axis=1, tiled=True)
    grad_out16 = jnp.dot(full_grad, out_proj, preferred_element_type=jnp.float32).astype(
        jnp.bfloat16
    )
    query_heads = split_heads(query_all)
    grad_heads = split_heads(grad_out16)
    grad_wide = grad_heads.astype(jnp.float32)
    heads_here = query_heads.shape[1]
    start_max = jnp.full((heads_here, frames), -1e30, jnp.float32)
    zeros_sum = jnp.zeros((heads_here, frames), jnp.float32)
    zeros_acc = jnp.zeros((heads_here, frames, HEAD_DIM), jnp.float32)
    zeros_keys = jnp.zeros((frames, heads_here, HEAD_DIM), jnp.float32)

    def masked_scores(key_rows, first_row):
        scores = (
            jnp.einsum(
                "qhd,khd->hqk",
                query_heads,
                split_heads(key_rows),
                preferred_element_type=jnp.float32,
            )
            * score_scale
        )
        key_ok = first_row + jnp.arange(key_rows.shape[0], dtype=jnp.int32) < valid_total
        return jnp.where(key_ok[None, None, :], scores, -jnp.inf)

    def forward_step(running, members, first_row):
        maxima, totals, numer = running
        key_rows, value_rows = members
        scores = masked_scores(key_rows, first_row)
        new_max = jnp.maximum(maxima, jnp.max(scores, axis=-1))
        shrink = jnp.exp(maxima - new_max)
        weights = jnp.exp(scores - new_max[..., None])
        totals = totals * shrink + jnp.sum(weights, axis=-1)
        numer = numer * shrink[..., None] + jnp.einsum(
            "hqk,khd->hqd",
            weights.astype(jnp.bfloat16),
            split_heads(value_rows),
            preferred_element_type=jnp.float32,
        )
        return (new_max, totals, numer)

    maxima, totals, numer = over_blocks(
        forward_step,
        (start_max, zeros_sum, zeros_acc),
        (
            lax.all_gather(key_all, "ctx", axis=0, tiled=True),
            lax.all_gather(value_all, "ctx", axis=0, tiled=True),
        ),
    )
    attn_out = numer / totals[..., None]
    log_total = maxima + jnp.log(totals)
    row_delta = jnp.einsum("qhd,hqd->hq", grad_wide, attn_out)
    query_sum = None

    def query_step(running, members, first_row):
        key_rows, value_rows = members
        scores = masked_scores(key_rows, first_row)
        probs = jnp.exp(scores - log_total[..., None])
        slopes = jnp.einsum(
            "qhd,khd->hqk", grad_heads, split_heads(value_rows), preferred_element_type=jnp.float32
        )
        dscores = probs * (slopes - row_delta[..., None])
        return running + jnp.einsum(
            "hqk,khd->hqd",
            dscores,
            split_heads(key_rows).astype(jnp.float32),
            precision=lax.Precision.HIGHEST,
        )

    query_sum = over_blocks(
        query_step,
        zeros_acc,
        (
            lax.all_gather(key_all, "ctx", axis=0, tiled=True),
            lax.all_gather(value_all, "ctx", axis=0, tiled=True),
        ),
    )
    lse_all, delta_all = (
        lax.all_gather(log_total, "ctx", axis=1, tiled=True),
        lax.all_gather(row_delta, "ctx", axis=1, tiled=True),
    )
    key_heads = split_heads(key_all)
    value_heads = split_heads(value_all)

    def key_step(running, members, first_row):
        key_acc, value_acc = running
        query_rows, grad_rows = members
        rows_here = query_rows.shape[0]
        lse_rows = lax.dynamic_slice_in_dim(lse_all, first_row, rows_here, 1)
        delta_rows = lax.dynamic_slice_in_dim(delta_all, first_row, rows_here, 1)
        scores = (
            jnp.einsum(
                "qhd,khd->hqk",
                split_heads(query_rows),
                key_heads,
                preferred_element_type=jnp.float32,
            )
            * score_scale
        )
        scores = jnp.where(frame_ok[None, None, :], scores, -jnp.inf)
        probs = jnp.exp(scores - lse_rows[..., None])
        probs16 = probs.astype(jnp.bfloat16)
        slopes = jnp.einsum(
            "qhd,khd->hqk", split_heads(grad_rows), value_heads, preferred_element_type=jnp.float32
        )
        dscores16 = (probs * (slopes - delta_rows[..., None])).astype(jnp.bfloat16)
        key_acc = key_acc + jnp.einsum(
            "hqk,qhd->khd", dscores16, split_heads(query_rows), preferred_element_type=jnp.float32
        )
        value_acc = value_acc + jnp.einsum(
            "hqk,qhd->khd", probs16, split_heads(grad_rows), preferred_element_type=jnp.float32
        )
        return (key_acc, value_acc)

    key_sum, value_sum = over_blocks(
        key_step,
        (zeros_keys, zeros_keys),
        (
            lax.all_gather(query_all, "ctx", axis=0, tiled=True),
            lax.all_gather(grad_out16, "ctx", axis=0, tiled=True),
        ),
    )
    q_grad = join_heads(query_sum * score_scale).astype(jnp.bfloat16)
    attn16 = join_heads(attn_out).astype(jnp.bfloat16)
    k_grad = (key_sum * score_scale).reshape(frames, local_width).astype(jnp.bfloat16)
    v_grad = value_sum.reshape(frames, local_width).astype(jnp.bfloat16)
    out_proj_grad = lax.psum_scatter(
        jnp.einsum("ta,tb->ab", full_grad, attn16, preferred_element_type=jnp.float32),
        "ctx",
        scatter_dimension=0,
        tiled=True,
    )
    return (q_grad, k_grad, v_grad, x_grad, out_proj_grad, conv_weight_grad)


def solution(mesh):
    placed = (
        P("ctx", "head"),
        P("ctx", "head"),
        P("ctx", "head"),
        P("ctx", "head"),
        P("ctx", "head"),
        P(),
        P(None, "head"),
        P(None, "head"),
    )
    return jax.shard_map(
        on_device,
        mesh=mesh,
        in_specs=placed,
        out_specs=(
            P("ctx", "head"),
            P("ctx", "head"),
            P("ctx", "head"),
            P("ctx", "head"),
            P("ctx", "head"),
            P(None, "head"),
        ),
        check_vma=False,
    )
```

profile of v0, /device:TPU:0, one launch (start us, length us, event | category | flops | bytes accessed | tf_op | source)
XLA Modules:
  0.0 354.8 jit_solution(6739002948123425645)
XLA Ops:
  10.9 1.3 collective-permute-start.1
  12.2 6.1 %collective-permute-start = (bf16[15,256]{1,0:T(8,128)(2,1)}, bf16[15,256]{1,0:T(8,128)(2,1)}, u32[]{:S(2)}, u32[]{:S(2)}) collective-permute-start(bf16[15,256]{1,0:T(8,128)(2,1)} %get-tuple-element.482), channel_id=1, source_target_pairs={{0,4},{4,8},{8,12},{12,16},{16,20},{20,24},{24,28},{1,5},{5,9},{9,... | collective-permute-start | bytes 23048 | tf_op jit(solution)/shard_map/ppermute | solution.py:14
  20.4 32.4 %all_gather.26 = bf16[1024,256]{1,0:T(8,128)(2,1)S(1)} all-gather(bf16[128,256]{1,0:T(8,128)(2,1)S(1)} %copy-done.13), channel_id=1, replica_groups=mesh['ctx'=8,'head'=4] {'ctx'}, dimensions={0}, use_global_device_ids=true | all-gather | bytes 589824 | tf_op jit(solution)/shard_map/all_gather | solution.py:218
  52.8 31.2 %all_gather.23 = bf16[1024,256]{1,0:T(8,128)(2,1)S(1)} all-gather(bf16[128,256]{1,0:T(8,128)(2,1)S(1)} %copy-done.14), channel_id=1, replica_groups=mesh['ctx'=8,'head'=4] {'ctx'}, dimensions={0}, use_global_device_ids=true | all-gather | bytes 589824 | tf_op jit(solution)/shard_map/all_gather | solution.py:173
  84.8 31.2 %all_gather.24 = bf16[1024,256]{1,0:T(8,128)(2,1)S(1)} all-gather(bf16[128,256]{1,0:T(8,128)(2,1)S(1)} %copy-done.15), channel_id=1, replica_groups=mesh['ctx'=8,'head'=4] {'ctx'}, dimensions={0}, use_global_device_ids=true | all-gather | bytes 589824 | tf_op jit(solution)/shard_map/all_gather | solution.py:174
  116.2 9.9 %while.39 = (s32[]{:T(128)}, f32[4,128]{1,0:T(4,128)S(1)}, f32[4,128]{1,0:T(4,128)S(1)}, f32[4,128,64]{1,2,0:T(8,128)S(1)}, s32[2]{0:T(128)S(1)}, /*index=5*/s32...) while((s32[]{:T(128)}, f32[4,128]{1,0:T(4,128)S(1)}, ...), condition=%wide.region_4.5_spmd.clone, body=%wide.region_1.4_spmd.clone.sunk | while | flops 69045760 | bytes 5080357 | solution.py:39
  118.8 1.2 fusion.146
  123.7 1.2 fusion.146
  126.8 1.6 copy.44
  129.1 26.8 %all_gather.27 = f32[4,1024]{1,0:T(4,128)} all-gather(f32[4,128]{1,0:T(4,128)S(1)} %log_add_fusion), channel_id=1, replica_groups=mesh['ctx'=8,'head'=4] {'ctx'}, dimensions={1}, use_global_device_ids=true | all-gather | bytes 18432 | tf_op jit(solution)/shard_map/all_gather | solution.py:178
  159.0 1.3 collective-permute-start.3
  160.3 4.5 %collective-permute-start.2 = (bf16[15,256]{1,0:T(8,128)(2,1)S(1)}, bf16[15,256]{1,0:T(8,128)(2,1)S(1)}, u32[]{:S(2)}, u32[]{:S(2)}) collective-permute-start(bf16[15,256]{1,0:T(8,128)(2,1)S(1)} %get-tuple-element.480), channel_id=1, source_target_pairs={{0,4},{4,8},{8,12},{12,16},{16,20},{20,24},{24,28},{1,5},{5,9},{9,... | collective-permute-start | bytes 23048 | tf_op jit(solution)/shard_map/ppermute | solution.py:14
  164.9 34.5 %psum.7 = f32[31,256]{1,0:T(8,128)} all-reduce(f32[31,256]{1,0:T(8,128)S(1)} %stack.127), channel_id=1, replica_groups=mesh['ctx'=8,'head'=4] {'ctx'}, use_global_device_ids=true, to_apply=%region_41.42 | all-reduce | flops 7936 | bytes 63488 | tf_op jit(solution)/shard_map/psum | solution.py:94
  201.2 5.8 %all_gather.25 = bf16[128,1024]{1,0:T(8,128)(2,1)S(1)} all-gather(bf16[128,256]{1,0:T(8,128)(2,1)S(1)} %fusion.26), channel_id=1, replica_groups=mesh['ctx'=8,'head'=4] {'head'}, dimensions={1}, use_global_device_ids=true | all-gather | bytes 327680 | tf_op jit(solution)/shard_map/all_gather | solution.py:99
  208.6 33.5 %all_gather.28 = bf16[1024,256]{1,0:T(8,128)(2,1)} all-gather(bf16[128,256]{1,0:T(8,128)(2,1)S(1)} %convolution_convert_fusion), channel_id=1, replica_groups=mesh['ctx'=8,'head'=4] {'ctx'}, dimensions={0}, use_global_device_ids=true | all-gather | bytes 589824 | tf_op jit(solution)/shard_map/all_gather | solution.py:219
  242.2 1.5 fusion.90
  243.6 27.0 %all_gather.29 = f32[4,1024]{1,0:T(4,128)} all-gather(f32[4,128]{1,0:T(4,128)S(1)} %get-tuple-element.773), channel_id=1, replica_groups=mesh['ctx'=8,'head'=4] {'ctx'}, dimensions={1}, use_global_device_ids=true | all-gather | bytes 18432 | tf_op jit(solution)/shard_map/all_gather | solution.py:179
  270.6 12.2 %while.40 = (s32[]{:T(128)}, f32[4,128,64]{1,2,0:T(8,128)}, s32[2]{0:T(128)S(1)}, s32[]{:T(128)}, bf16[2,512,256]{1,2,0:T(8,128)(2,1)S(1)}, /*index=5*/bf16[128,...) while((s32[]{:T(128)}, f32[4,128,64]{1,2,0:T(8,128)}, ...), condition=%wide.region_6.7_spmd.clone, body=%wide.region_5.6_spmd.clone.sunk | while | flops 269812736 | bytes 6427827 | solution.py:39
  272.6 1.3 fusion.155
  273.9 1.2 fusion.156
  275.1 1.2 convolution_add_fusion.5
  278.2 1.3 fusion.155
  279.5 1.2 fusion.156
  280.7 2.1 convolution_add_fusion.5
  284.6 1.3 fusion.97
  286.0 1.0 copy-done.1
  287.0 13.6 %while.41 = (s32[]{:T(128)}, f32[128,4,64]{0,2,1:T(8,128)S(1)}, f32[128,4,64]{0,2,1:T(8,128)}, bf16[2,512,256]{2,1,0:T(8,128)(2,1)S(1)}, bf16[128,4,64]{0,2,1:T(...) while((s32[]{:T(128)}, f32[128,4,64]{0,2,1:T(8,128)S(1)}, ...), condition=%wide.region_8.9_spmd.clone, body=%wide.region_7.8_spmd.clone.sunk | while | flops 136184064 | bytes 8045098 | solution.py:39
  289.8 1.3 fusion.164
  291.3 1.5 fusion.165
  296.6 1.3 fusion.164
  298.1 1.6 fusion.165
  302.3 45.7 %reduce-scatter.2.cloned.1.call-done = f32[128,256]{1,0:T(8,128)} async-done(((f32[1024,256]{1,0:T(8,128)}), f32[128,256]{1,0:T(8,128)}) %reduce-scatter.2.cloned.1.call-update) | async-done | bytes 131088 | tf_op jit(solution)/shard_map/reduce_scatter | solution.py:226
  (192 shorter events, 32.7 us)
Async XLA Ops:
  7.2 200.5 %copy-start = (bf16[1024,256]{1,0:T(8,128)(2,1)S(1)}, bf16[1024,256]{1,0:T(8,128)(2,1)}, u32[]{:S(2)}) copy-start(bf16[1024,256]{1,0:T(8,128)(2,1)} %param.20) | copy-start | bytes 1572868
  7.2 340.7 %reduce-scatter.2.cloned.1.call-start = ((), (), s32[]{:S(2)}) async-start(), calls=%async_computation.1 | async-start | bytes 1179648 | tf_op jit(solution)/shard_map/reduce_scatter | solution.py:226
  9.4 9.0 %copy-start.18 = (bf16[31,256]{1,0:T(8,128)(2,1)S(1)}, bf16[31,256]{1,0:T(8,128)(2,1)}, u32[]{:S(2)}) copy-start(bf16[31,256]{1,0:T(8,128)(2,1)} %param.21) | copy-start | bytes 47620
  10.3 9.3 %copy-start.9 = (bf16[128,256]{1,0:T(8,128)(2,1)}, bf16[128,256]{1,0:T(8,128)(2,1)S(1)}, u32[]{:S(2)}) copy-start(bf16[128,256]{1,0:T(8,128)(2,1)S(1)} %broadcast_select_fusion) | copy-start | bytes 196612
  10.3 9.3 %copy-start.13 = (bf16[128,256]{1,0:T(8,128)(2,1)S(1)}, bf16[128,256]{1,0:T(8,128)(2,1)}, u32[]{:S(2)}) copy-start(bf16[128,256]{1,0:T(8,128)(2,1)} %param.14) | copy-start | bytes 196612
  10.9 145.0 %collective-permute-start.1 = (bf16[15,256]{1,0:T(8,128)(2,1)}, bf16[15,256]{1,0:T(8,128)(2,1)}, u32[]{:S(2)}, u32[]{:S(2)}) collective-permute-start(bf16[15,256]{1,0:T(8,128)(2,1)} %get-tuple-element.483), channel_id=1, source_target_pairs={{4,0},{8,4},{12,8},{16,12},{20,16},{24,20},{28,24},{5,1},{9,5},{13... | collective-permute-start | bytes 23048 | tf_op jit(solution)/shard_map/ppermute | solution.py:17
  12.2 143.7 %collective-permute-start = (bf16[15,256]{1,0:T(8,128)(2,1)}, bf16[15,256]{1,0:T(8,128)(2,1)}, u32[]{:S(2)}, u32[]{:S(2)}) collective-permute-start(bf16[15,256]{1,0:T(8,128)(2,1)} %get-tuple-element.482), channel_id=1, source_target_pairs={{0,4},{4,8},{8,12},{12,16},{16,20},{20,24},{24,28},{1,5},{5,9},{9,... | collective-permute-start | bytes 23048 | tf_op jit(solution)/shard_map/ppermute | solution.py:14
  20.4 32.4 %copy-start.14 = (bf16[128,256]{1,0:T(8,128)(2,1)S(1)}, bf16[128,256]{1,0:T(8,128)(2,1)}, u32[]{:S(2)}) copy-start(bf16[128,256]{1,0:T(8,128)(2,1)} %param.15) | copy-start | bytes 196612
  126.8 1.6 copy-start.16
  128.4 27.6 %copy-start.10 = (bf16[128,256]{1,0:T(8,128)(2,1)S(1)}, bf16[128,256]{1,0:T(8,128)(2,1)}, u32[]{:S(2)}) copy-start(bf16[128,256]{1,0:T(8,128)(2,1)} %copy-done.9) | copy-start | bytes 196612
  156.0 1.1 copy-start.20
  156.0 1.1 copy-start.21
  156.0 1.1 copy-start.22
  156.0 1.1 copy-start.23
  156.0 1.1 copy-start.24
  156.0 1.1 copy-start.25
  156.0 1.1 copy-start.26
  156.0 1.1 copy-start.27
  156.1 1.1 copy-start.28
  156.1 1.1 copy-start.29
  156.1 1.1 copy-start.30
  156.1 1.1 copy-start.31
  156.1 1.1 copy-start.32
  156.1 1.1 copy-start.33
  156.1 1.1 copy-start.34
  156.1 1.1 copy-start.35
  159.0 40.5 %collective-permute-start.3 = (bf16[15,256]{1,0:T(8,128)(2,1)S(1)}, bf16[15,256]{1,0:T(8,128)(2,1)S(1)}, u32[]{:S(2)}, u32[]{:S(2)}) collective-permute-start(bf16[15,256]{1,0:T(8,128)(2,1)S(1)} %get-tuple-element.481), channel_id=1, source_target_pairs={{4,0},{8,4},{12,8},{16,12},{20,16},{24,20},{28,24},{5,1},{9,5},{13... | collective-permute-start | bytes 23048 | tf_op jit(solution)/shard_map/ppermute | solution.py:17
  160.3 39.2 %collective-permute-start.2 = (bf16[15,256]{1,0:T(8,128)(2,1)S(1)}, bf16[15,256]{1,0:T(8,128)(2,1)S(1)}, u32[]{:S(2)}, u32[]{:S(2)}) collective-permute-start(bf16[15,256]{1,0:T(8,128)(2,1)S(1)} %get-tuple-element.480), channel_id=1, source_target_pairs={{0,4},{4,8},{8,12},{12,16},{16,20},{20,24},{24,28},{1,5},{5,9},{9,... | collective-permute-start | bytes 23048 | tf_op jit(solution)/shard_map/ppermute | solution.py:14
  208.6 33.5 %copy-start.6 = (f32[4,128,64]{1,2,0:T(8,128)S(1)}, f32[4,128,64]{1,2,0:T(8,128)}, u32[]{:S(2)}) copy-start(f32[4,128,64]{1,2,0:T(8,128)} %copy-done.5) | copy-start | bytes 393220
  282.8 1.7 copy-start.8
  291.3 1.6 copy-start.2
  298.1 1.6 copy-start.2
  (31 other events, 27.1 us)
Sparse Core Ops, SparseCore 0:
  286.1 61.7 reduce-scatter.1
where the time goes:
time: 356 us; the launch traced here: 355 us
  blocking collectives  222 us (62%)
  waiting for transfers between devices  45.7 us (13%)
  local copies, waits for them, and re-layouts  23.8 us (7%)
  matrix products  19.1 us (5%)
  between operations  14.7 us (4%)
  starting transfers between devices  13.3 us (4%)
  other arithmetic  11.6 us (3%)
  loops' own time  4.23 us (1%)
    reduce_scatter x1, waiting for transfers between devices, on_device(): lax.psum_scatter(jnp.einsum('ta,tb->ab', full_grad, attn16, preferred_ele...  45.7 us
    psum x1, blocking collectives, on_device(): conv_weight_grad = lax.psum(tap_products(grad_conv, input_ext), 'ctx')  34.5 us
    all_gather x1, blocking collectives, on_device(): lax.all_gather(grad_out16, 'ctx', axis=0, tiled=True)  33.5 us
    all_gather x1, blocking collectives, on_device(): lax.all_gather(query_all, 'ctx', axis=0, tiled=True)  32.4 us
    all_gather x1, blocking collectives, on_device(): lax.all_gather(value_all, 'ctx', axis=0, tiled=True)  31.2 us
    all_gather x1, blocking collectives, on_device(): lax.all_gather(key_all, 'ctx', axis=0, tiled=True)  31.2 us
    all_gather x1, blocking collectives, on_device(): lax.all_gather(row_delta, 'ctx', axis=1, tiled=True)  27 us
    all_gather x1, blocking collectives, on_device(): lax.all_gather(log_total, 'ctx', axis=1, tiled=True)  26.8 us
  transfers between devices with their start and end apart: 5, of which 1 were waited for; matrix products, arithmetic and copies ran while one was open for 7% of the time, Pallas kernels for 0%

commit v1 on v0

--- a/solution.py
+++ b/solution.py
@@ -91,7 +91,7 @@
     conv_out = conv_forward(input_ext, conv_weight, frames)
     grad_conv = gate_slope(conv_out, cotangent)
     grad_ext = extended_2(grad_conv, (("ctx", 0),), half_taps)
-    conv_weight_grad = lax.psum(tap_products(grad_conv, input_ext), "ctx")
+    conv_weight_grad = jnp.sum(lax.all_gather(tap_products(grad_conv, input_ext), "ctx"), axis=0)
     grad_input = conv_backward(grad_ext, conv_weight, frames)
     x_grad = (cotangent.astype(jnp.float32) + jnp.where(frame_ok[:, None], grad_input, 0.0)).astype(
         jnp.bfloat16

time: 356 us -> 353 us (level)
    psum x1 -> x0, blocking collectives: 34.5 us -> none  [on_device(): conv_weight_grad = lax.psum(tap_products(grad_conv, input_ext), 'ctx')]
    all_gather x0 -> x1, blocking collectives: none -> 30.9 us  [on_device(): lax.all_gather(tap_products(grad_conv, input_ext), 'ctx')]
where the time goes in v1:
time: 353 us; the launch traced here: 352 us
  blocking collectives  219 us (62%)
  waiting for transfers between devices  45.6 us (13%)
  local copies, waits for them, and re-layouts  23.8 us (7%)
  matrix products  19.1 us (5%)
  between operations  14.7 us (4%)
  starting transfers between devices  13.3 us (4%)
  other arithmetic  12.3 us (3%)
  loops' own time  4.23 us (1%)
    reduce_scatter x1, waiting for transfers between devices, on_device(): lax.psum_scatter(jnp.einsum('ta,tb->ab', full_grad, attn16, preferred_ele...  45.6 us
    all_gather x1, blocking collectives, on_device(): lax.all_gather(grad_out16, 'ctx', axis=0, tiled=True)  33.5 us
    all_gather x1, blocking collectives, on_device(): lax.all_gather(query_all, 'ctx', axis=0, tiled=True)  32.4 us
    all_gather x1, blocking collectives, on_device(): lax.all_gather(value_all, 'ctx', axis=0, tiled=True)  31.2 us
    all_gather x1, blocking collectives, on_device(): lax.all_gather(key_all, 'ctx', axis=0, tiled=True)  31.2 us
    all_gather x1, blocking collectives, on_device(): lax.all_gather(tap_products(grad_conv, input_ext), 'ctx')  30.9 us
    all_gather x1, blocking collectives, on_device(): lax.all_gather(row_delta, 'ctx', axis=1, tiled=True)  27 us
    all_gather x1, blocking collectives, on_device(): lax.all_gather(log_total, 'ctx', axis=1, tiled=True)  26.8 us
  transfers between devices with their start and end apart: 5, of which 1 were waited for; matrix products, arithmetic and copies ran while one was open for 7% of the time, Pallas kernels for 0%

profile of v1, /device:TPU:0, one launch (start us, length us, event | category | flops | bytes accessed | tf_op | source)
XLA Modules:
  0.0 351.7 jit_solution(7023921871371628992)
XLA Ops:
  10.9 1.3 collective-permute-start.1
  12.2 6.1 %collective-permute-start = (bf16[15,256]{1,0:T(8,128)(2,1)}, bf16[15,256]{1,0:T(8,128)(2,1)}, u32[]{:S(2)}, u32[]{:S(2)}) collective-permute-start(bf16[15,256]{1,0:T(8,128)(2,1)} %get-tuple-element.519), channel_id=1, source_target_pairs={{0,4},{4,8},{8,12},{12,16},{16,20},{20,24},{24,28},{1,5},{5,9},{9,... | collective-permute-start | bytes 23048 | tf_op jit(solution)/shard_map/ppermute | solution.py:14
  20.4 32.4 %all_gather.32 = bf16[1024,256]{1,0:T(8,128)(2,1)S(1)} all-gather(bf16[128,256]{1,0:T(8,128)(2,1)S(1)} %copy-done.13), channel_id=1, replica_groups=mesh['ctx'=8,'head'=4] {'ctx'}, dimensions={0}, use_global_device_ids=true | all-gather | bytes 589824 | tf_op jit(solution)/shard_map/all_gather | solution.py:218
  52.8 31.2 %all_gather.29 = bf16[1024,256]{1,0:T(8,128)(2,1)S(1)} all-gather(bf16[128,256]{1,0:T(8,128)(2,1)S(1)} %copy-done.14), channel_id=1, replica_groups=mesh['ctx'=8,'head'=4] {'ctx'}, dimensions={0}, use_global_device_ids=true | all-gather | bytes 589824 | tf_op jit(solution)/shard_map/all_gather | solution.py:173
  84.8 31.2 %all_gather.30 = bf16[1024,256]{1,0:T(8,128)(2,1)S(1)} all-gather(bf16[128,256]{1,0:T(8,128)(2,1)S(1)} %copy-done.15), channel_id=1, replica_groups=mesh['ctx'=8,'head'=4] {'ctx'}, dimensions={0}, use_global_device_ids=true | all-gather | bytes 589824 | tf_op jit(solution)/shard_map/all_gather | solution.py:174
  116.2 9.9 %while.39 = (s32[]{:T(128)}, f32[4,128]{1,0:T(4,128)S(1)}, f32[4,128]{1,0:T(4,128)S(1)}, f32[4,128,64]{1,2,0:T(8,128)S(1)}, s32[2]{0:T(128)S(1)}, /*index=5*/s32...) while((s32[]{:T(128)}, f32[4,128]{1,0:T(4,128)S(1)}, ...), condition=%wide.region_4.5_spmd.clone, body=%wide.region_1.4_spmd.clone.sunk | while | flops 69045760 | bytes 5080357 | solution.py:39
  118.8 1.2 fusion.146
  123.7 1.2 fusion.146
  126.8 1.6 copy.58
  129.1 26.8 %all_gather.33 = f32[4,1024]{1,0:T(4,128)} all-gather(f32[4,128]{1,0:T(4,128)S(1)} %log_add_fusion), channel_id=1, replica_groups=mesh['ctx'=8,'head'=4] {'ctx'}, dimensions={1}, use_global_device_ids=true | all-gather | bytes 18432 | tf_op jit(solution)/shard_map/all_gather | solution.py:178
  159.0 1.3 collective-permute-start.3
  160.3 4.5 %collective-permute-start.2 = (bf16[15,256]{1,0:T(8,128)(2,1)S(1)}, bf16[15,256]{1,0:T(8,128)(2,1)S(1)}, u32[]{:S(2)}, u32[]{:S(2)}) collective-permute-start(bf16[15,256]{1,0:T(8,128)(2,1)S(1)} %get-tuple-element.517), channel_id=1, source_target_pairs={{0,4},{4,8},{8,12},{12,16},{16,20},{20,24},{24,28},{1,5},{5,9},{9,... | collective-permute-start | bytes 23048 | tf_op jit(solution)/shard_map/ppermute | solution.py:14
  164.9 30.9 %all-gather.1 = f32[8,31,256]{2,1,0:T(8,128)S(1)} all-gather(f32[1,31,256]{2,1,0:T(8,128)S(1)} %bitcast.192), channel_id=2, replica_groups=mesh['ctx'=8,'head'=4] {'ctx'}, dimensions={0}, use_global_device_ids=true | all-gather | bytes 285696 | tf_op jit(solution)/shard_map/all_gather | solution.py:94
  198.2 5.8 %all_gather.31 = bf16[128,1024]{1,0:T(8,128)(2,1)S(1)} all-gather(bf16[128,256]{1,0:T(8,128)(2,1)S(1)} %fusion.26), channel_id=1, replica_groups=mesh['ctx'=8,'head'=4] {'head'}, dimensions={1}, use_global_device_ids=true | all-gather | bytes 327680 | tf_op jit(solution)/shard_map/all_gather | solution.py:99
  205.6 33.5 %all_gather.34 = bf16[1024,256]{1,0:T(8,128)(2,1)} all-gather(bf16[128,256]{1,0:T(8,128)(2,1)S(1)} %convolution_convert_fusion), channel_id=1, replica_groups=mesh['ctx'=8,'head'=4] {'ctx'}, dimensions={0}, use_global_device_ids=true | all-gather | bytes 589824 | tf_op jit(solution)/shard_map/all_gather | solution.py:219
  239.1 1.5 fusion.90
  240.6 27.0 %all_gather.35 = f32[4,1024]{1,0:T(4,128)} all-gather(f32[4,128]{1,0:T(4,128)S(1)} %get-tuple-element.810), channel_id=1, replica_groups=mesh['ctx'=8,'head'=4] {'ctx'}, dimensions={1}, use_global_device_ids=true | all-gather | bytes 18432 | tf_op jit(solution)/shard_map/all_gather | solution.py:179
  267.6 12.2 %while.40 = (s32[]{:T(128)}, f32[4,128,64]{1,2,0:T(8,128)}, s32[2]{0:T(128)S(1)}, s32[]{:T(128)}, bf16[2,512,256]{1,2,0:T(8,128)(2,1)S(1)}, /*index=5*/bf16[128,...) while((s32[]{:T(128)}, f32[4,128,64]{1,2,0:T(8,128)}, ...), condition=%wide.region_6.7_spmd.clone, body=%wide.region_5.6_spmd.clone.sunk | while | flops 269812736 | bytes 6427827 | solution.py:39
  269.5 1.3 fusion.155
  270.8 1.2 fusion.156
  272.0 1.2 convolution_add_fusion.5
  275.2 1.3 fusion.155
  276.4 1.2 fusion.156
  277.6 2.1 convolution_add_fusion.5
  281.5 1.3 fusion.97
  282.9 1.0 copy-done.1
  283.9 13.6 %while.41 = (s32[]{:T(128)}, f32[128,4,64]{0,2,1:T(8,128)S(1)}, f32[128,4,64]{0,2,1:T(8,128)}, bf16[2,512,256]{2,1,0:T(8,128)(2,1)S(1)}, bf16[128,4,64]{0,2,1:T(...) while((s32[]{:T(128)}, f32[128,4,64]{0,2,1:T(8,128)S(1)}, ...), condition=%wide.region_8.9_spmd.clone, body=%wide.region_7.8_spmd.clone.sunk | while | flops 136184064 | bytes 8045098 | solution.py:39
  286.7 1.3 fusion.164
  288.3 1.6 fusion.165
  293.6 1.3 fusion.164
  295.1 1.6 fusion.165
  299.2 45.6 %reduce-scatter.2.cloned.1.call-done = f32[128,256]{1,0:T(8,128)} async-done(((f32[1024,256]{1,0:T(8,128)}), f32[128,256]{1,0:T(8,128)}) %reduce-scatter.2.cloned.1.call-update) | async-done | bytes 131088 | tf_op jit(solution)/shard_map/reduce_scatter | solution.py:226
  (193 shorter events, 33.3 us)
Async XLA Ops:
  7.2 197.5 %copy-start = (bf16[1024,256]{1,0:T(8,128)(2,1)S(1)}, bf16[1024,256]{1,0:T(8,128)(2,1)}, u32[]{:S(2)}) copy-start(bf16[1024,256]{1,0:T(8,128)(2,1)} %param.20) | copy-start | bytes 1572868
  7.2 337.6 %reduce-scatter.2.cloned.1.call-start = ((), (), s32[]{:S(2)}) async-start(), calls=%async_computation.1 | async-start | bytes 1179648 | tf_op jit(solution)/shard_map/reduce_scatter | solution.py:226
  9.4 9.0 %copy-start.18 = (bf16[31,256]{1,0:T(8,128)(2,1)S(1)}, bf16[31,256]{1,0:T(8,128)(2,1)}, u32[]{:S(2)}) copy-start(bf16[31,256]{1,0:T(8,128)(2,1)} %param.21) | copy-start | bytes 47620
  10.3 9.3 %copy-start.9 = (bf16[128,256]{1,0:T(8,128)(2,1)}, bf16[128,256]{1,0:T(8,128)(2,1)S(1)}, u32[]{:S(2)}) copy-start(bf16[128,256]{1,0:T(8,128)(2,1)S(1)} %broadcast_select_fusion) | copy-start | bytes 196612
  10.3 9.3 %copy-start.13 = (bf16[128,256]{1,0:T(8,128)(2,1)S(1)}, bf16[128,256]{1,0:T(8,128)(2,1)}, u32[]{:S(2)}) copy-start(bf16[128,256]{1,0:T(8,128)(2,1)} %param.14) | copy-start | bytes 196612
  10.9 145.0 %collective-permute-start.1 = (bf16[15,256]{1,0:T(8,128)(2,1)}, bf16[15,256]{1,0:T(8,128)(2,1)}, u32[]{:S(2)}, u32[]{:S(2)}) collective-permute-start(bf16[15,256]{1,0:T(8,128)(2,1)} %get-tuple-element.520), channel_id=1, source_target_pairs={{4,0},{8,4},{12,8},{16,12},{20,16},{24,20},{28,24},{5,1},{9,5},{13... | collective-permute-start | bytes 23048 | tf_op jit(solution)/shard_map/ppermute | solution.py:17
  12.2 143.7 %collective-permute-start = (bf16[15,256]{1,0:T(8,128)(2,1)}, bf16[15,256]{1,0:T(8,128)(2,1)}, u32[]{:S(2)}, u32[]{:S(2)}) collective-permute-start(bf16[15,256]{1,0:T(8,128)(2,1)} %get-tuple-element.519), channel_id=1, source_target_pairs={{0,4},{4,8},{8,12},{12,16},{16,20},{20,24},{24,28},{1,5},{5,9},{9,... | collective-permute-start | bytes 23048 | tf_op jit(solution)/shard_map/ppermute | solution.py:14
  20.4 32.4 %copy-start.14 = (bf16[128,256]{1,0:T(8,128)(2,1)S(1)}, bf16[128,256]{1,0:T(8,128)(2,1)}, u32[]{:S(2)}) copy-start(bf16[128,256]{1,0:T(8,128)(2,1)} %param.15) | copy-start | bytes 196612
  126.8 1.6 copy-start.16
  128.4 27.6 %copy-start.10 = (bf16[128,256]{1,0:T(8,128)(2,1)S(1)}, bf16[128,256]{1,0:T(8,128)(2,1)}, u32[]{:S(2)}) copy-start(bf16[128,256]{1,0:T(8,128)(2,1)} %copy-done.9) | copy-start | bytes 196612
  156.0 1.1 copy-start.20
  156.0 1.1 copy-start.21
  156.0 1.1 copy-start.22
  156.0 1.1 copy-start.23
  156.0 1.1 copy-start.24
  156.0 1.1 copy-start.25
  156.0 1.1 copy-start.26
  156.0 1.1 copy-start.27
  156.0 1.1 copy-start.28
  156.1 1.1 copy-start.29
  156.1 1.1 copy-start.30
  156.1 1.1 copy-start.31
  156.1 1.1 copy-start.32
  156.1 1.1 copy-start.33
  156.1 1.1 copy-start.34
  156.1 1.1 copy-start.35
  159.0 37.5 %collective-permute-start.3 = (bf16[15,256]{1,0:T(8,128)(2,1)S(1)}, bf16[15,256]{1,0:T(8,128)(2,1)S(1)}, u32[]{:S(2)}, u32[]{:S(2)}) collective-permute-start(bf16[15,256]{1,0:T(8,128)(2,1)S(1)} %get-tuple-element.518), channel_id=1, source_target_pairs={{4,0},{8,4},{12,8},{16,12},{20,16},{24,20},{28,24},{5,1},{9,5},{13... | collective-permute-start | bytes 23048 | tf_op jit(solution)/shard_map/ppermute | solution.py:17
  160.3 36.2 %collective-permute-start.2 = (bf16[15,256]{1,0:T(8,128)(2,1)S(1)}, bf16[15,256]{1,0:T(8,128)(2,1)S(1)}, u32[]{:S(2)}, u32[]{:S(2)}) collective-permute-start(bf16[15,256]{1,0:T(8,128)(2,1)S(1)} %get-tuple-element.517), channel_id=1, source_target_pairs={{0,4},{4,8},{8,12},{12,16},{16,20},{20,24},{24,28},{1,5},{5,9},{9,... | collective-permute-start | bytes 23048 | tf_op jit(solution)/shard_map/ppermute | solution.py:14
  205.6 33.5 %copy-start.6 = (f32[4,128,64]{1,2,0:T(8,128)S(1)}, f32[4,128,64]{1,2,0:T(8,128)}, u32[]{:S(2)}) copy-start(f32[4,128,64]{1,2,0:T(8,128)} %copy-done.5) | copy-start | bytes 393220
  279.7 1.7 copy-start.8
  288.3 1.6 copy-start.2
  295.1 1.6 copy-start.2
  (31 other events, 27.1 us)
Sparse Core Ops, SparseCore 0:
  283.0 61.7 reduce-scatter.1
